TPU v7x, 32 devices: a whole 2x2x4 slice. The times are simulated.
32 devices in a mesh: tile: 8 (over z, y), acq: 4 (over x, core).
Axes of the slice: x: 2, y: 2, z: 4, core: 2. Of those that a mesh axis runs over, the one named last changes fastest.
Arguments:
- phases: float32 [64, 131072], P('acq', 'tile'), may hold values from -6 to 6
- coherence: float32 [131072], P('tile'), may hold values from 0.1 to 1
- pixel_index: int32 [131072], P('tile'), may hold values from 0 to 8191
- send_list: int32 [64, 128], P('tile'), may hold values from 0 to 16383, as said below
- counts: int32 [8, 8], P('tile'), may hold values from 16 to 128, as said below
- band_width: int32 [64], replicated, may hold values from 1 to 8
Outputs:
- residual: float32 [64, 8192], P('acq', 'tile')
- screen: float32 [64, 64, 1024], P('acq', 'tile')
Inputs may be any that keep to these rules, and one draw needn't show every extreme that they name: `counts`: for every device two owner tiles (the same for all devices, possibly one) receive all 128 slots; the others receive between 16 and 63. `send_list`: the live entries of one device's rows are distinct local scatterer indices; entries beyond a row's count are valid indices that carry no data.
All inputs are finite; a program needn't handle non-finite values.
Results may differ from a plain program's by a relative error of at most 0.0003.
Values sent between devices are 32-bit elements; how exact they have to be, the bound alone decides.
No kernel may reach another device: no remote copies, remote signals or barrier semaphores. Data moves between devices by JAX's collectives and lax.ppermute only.
A program may use at most 64 MiB of HBM per device.

v0:
```python
import jax
import jax.numpy as jnp
from jax import lax
from jax.sharding import PartitionSpec as P

ACQ = 64
ROWS_DEV = 8
COLS = 1024
RADIUS = 4
SLAB_PIX = 8192
min_weight = 0.1


def with_halo(cells, sides, width):
    for axis, dim in sides:
        count = lax.axis_size(axis)
        ends = count - 1
        head = lax.slice_in_dim(cells, 0, width, axis=dim)
        tail = lax.slice_in_dim(cells, cells.shape[dim] - width, cells.shape[dim], axis=dim)
        cells = jnp.concatenate(
            [
                lax.ppermute(tail, axis, [(i, (i + 1) % count) for i in range(ends)]),
                cells,
                lax.ppermute(head, axis, [((i + 1) % count, i) for i in range(ends)]),
            ],
            axis=dim,
        )
    return cells


def temporal_matrix(band_width):
    positions = jnp.arange(ACQ, dtype=jnp.int32)
    lower = jnp.maximum(positions - band_width, 0)
    upper = jnp.minimum(positions + band_width, ACQ - 1)
    inside = (positions[None, :] >= lower[:, None]) & (positions[None, :] <= upper[:, None])
    window = (upper - lower + 1).astype(jnp.float32)
    return jnp.eye(ACQ, dtype=jnp.float32) - inside.astype(jnp.float32) / window[:, None]


def kernel_weights():
    return [
        (RADIUS + 1 - abs(offset - RADIUS)) / float((RADIUS + 1) ** 2)
        for offset in range(2 * RADIUS + 1)
    ]


def smooth(padded_rows):
    weights = kernel_weights()
    row_count = padded_rows.shape[-2] - 2 * RADIUS
    vertical = weights[0] * padded_rows[..., 0:row_count, :]
    for offset in range(1, 2 * RADIUS + 1):
        vertical = vertical + weights[offset] * padded_rows[..., offset : offset + row_count, :]
    column_count = vertical.shape[-1]
    pad_width = [(0, 0)] * (vertical.ndim - 1) + [(RADIUS, RADIUS)]
    widened = jnp.pad(vertical, pad_width)
    total = weights[0] * widened[..., 0:column_count]
    for offset in range(1, 2 * RADIUS + 1):
        total = total + weights[offset] * widened[..., offset : offset + column_count]
    return total


def apply_highpass(highpass, series):
    return jnp.dot(
        highpass, series, precision=lax.Precision.HIGHEST, preferred_element_type=jnp.float32
    )


def shards(phases, coherence, pixel_index, send_list, counts, band_width):
    acq_loc = phases.shape[0]
    capacity = send_list.shape[1]
    highpass = temporal_matrix(band_width)
    live_slot = jnp.arange(capacity, dtype=jnp.int32)[None, :] < counts[0][:, None]
    slot_weight = jnp.where(live_slot, coherence[send_list], jnp.float32(0.0))
    slot_pixel = pixel_index[send_list]
    outgoing = phases[:, send_list] * slot_weight[None]
    arrived, arrived_weight, arrived_pixel = (
        lax.all_to_all(outgoing, "tile", split_axis=1, concat_axis=1, tiled=True),
        lax.all_to_all(slot_weight[None], "tile", split_axis=1, concat_axis=1, tiled=True),
        lax.all_to_all(slot_pixel[None], "tile", split_axis=1, concat_axis=1, tiled=True),
    )
    targets = arrived_pixel.reshape(-1)
    phase_image = (
        jnp.zeros((acq_loc, SLAB_PIX), jnp.float32).at[:, targets].add(arrived.reshape(acq_loc, -1))
    )
    weight_sum = jnp.zeros((SLAB_PIX,), jnp.float32).at[targets].add(arrived_weight.reshape(-1))
    series = lax.all_to_all(phase_image, "acq", split_axis=1, concat_axis=0, tiled=True)
    phase_image = lax.all_to_all(
        apply_highpass(highpass, series), "acq", split_axis=0, concat_axis=1, tiled=True
    )
    stacked = jnp.concatenate([phase_image, weight_sum[None, :]], axis=0).reshape(
        acq_loc + 1, ROWS_DEV, COLS
    )
    padded = with_halo(stacked, (("tile", 1),), RADIUS)
    smoothed = smooth(padded)
    screen = smoothed[:acq_loc] / jnp.maximum(smoothed[acq_loc], min_weight)
    flattened = screen.reshape(acq_loc, SLAB_PIX)
    sampled = flattened[:, arrived_pixel[0]]
    returned = lax.all_to_all(sampled, "tile", split_axis=1, concat_axis=1, tiled=True)
    residual = jnp.where(live_slot[None], phases[:, send_list] - returned, jnp.float32(0.0))
    return (residual.reshape(acq_loc, -1), screen)


def solution(mesh):
    return jax.shard_map(
        shards,
        mesh=mesh,
        in_specs=(P("acq", "tile"), P("tile"), P("tile"), P("tile", None), P("tile", None), P()),
        out_specs=(P("acq", "tile"), P("acq", "tile", None)),
        check_vma=False,
    )
```

profile of v0, /device:TPU:0, one launch (start us, length us, event | category | flops | bytes accessed | tf_op | source)
XLA Modules:
  0.0 134.2 jit_solution(15241608124049495737)
XLA Ops:
  1.5 10.5 %gather_fusion.1 = s32[1024]{0:T(1024)} fusion(s32[16384]{0:T(1024)S(1)} %copy-done, s32[1024]{0:T(1024)S(1)} %fusion.58), kind=kCustom, calls=%fused_computation.1 | custom fusion | bytes 12288 | tf_op jit(solution)/shard_map/gather | solution.py:74
  12.0 7.3 %all-to-all-start = ((s32[1,8,128]{2,0,1:T(1,128)}), s32[1,8,128]{2,0,1:T(1,128)S(1)}, u32[]{:S(2)}, u32[]{:S(2)}) async-start(s32[1,8,128]{2,0,1:T(1,128)} %bitcast.5), calls=%async_computation | async-start | bytes 8192 | tf_op jit(solution)/shard_map/all_to_all | solution.py:79
  19.3 6.2 %gather_fusion.2 = f32[1024]{0:T(1024)S(1)} fusion(f32[16384]{0:T(1024)S(1)} %copy-done.1, s32[1024]{0:T(1024)S(1)} %fusion.58), kind=kCustom, calls=%fused_computation.2 | custom fusion | bytes 12288 | tf_op jit(solution)/shard_map/gather | solution.py:73
  25.5 4.6 %copy.23 = f32[16,16384]{0,1:T(8,128)} copy(f32[16,16384]{1,0:T(8,128)S(1)} %copy-done.3) | data formatting | bytes 2097152 | tf_op args[0]
  30.1 6.2 %gather_fusion = f32[1024,16]{1,0:T(8,128)S(1)} fusion(f32[16,16384]{0,1:T(8,128)} %copy.23, s32[1024]{0:T(1024)S(1)} %fusion.58), kind=kCustom, calls=%fused_computation | custom fusion | bytes 135168 | tf_op jit(solution)/shard_map/gather | solution.py:99
  37.2 6.0 %all-to-all-start.1 = ((f32[16,8,128]{2,0,1:T(8,128)}), f32[16,8,128]{2,0,1:T(8,128)S(1)}, u32[]{:S(2)}, u32[]{:S(2)}) async-start(f32[16,8,128]{2,0,1:T(8,128)} %bitcast_multiply_fusion), calls=%async_computation.1 | async-start | bytes 131072 | tf_op jit(solution)/shard_map/all_to_all | solution.py:77
  43.2 6.9 %all-to-all-done.1 = f32[16,8,128]{2,0,1:T(8,128)S(1)} async-done(((f32[16,8,128]{2,0,1:T(8,128)}), f32[16,8,128]{2,0,1:T(8,128)S(1)}, u32[]{:S(2)}, u32[]{:S(2)}) %all-to-all-start.1) | async-done | bytes 65568 | tf_op jit(solution)/shard_map/all_to_all | solution.py:77
  50.3 8.2 %scatter_custom_fusion = f32[16,8192]{0,1:T(8,128)} fusion(s32[1024]{0:T(1024)S(1)} %bitcast.63, f32[1024,16]{1,0:T(8,128)S(1)} %copy.26, f32[]{:T(128)} %constant.2.clone.1), kind=kCustom, calls=%fused_computation.6 | custom fusion | flops 16384 | bytes 524292 | tf_op jit(solution)/shard_map/scatter-add | solution.py:83
  58.5 3.5 %copy.27 = f32[16,4,2048]{2,0,1:T(8,128)} copy(f32[16,4,2048]{0,2,1:T(8,128)} %bitcast.55) | data formatting | bytes 1048576 | tf_op jit(solution)/shard_map/all_to_all | solution.py:86
  62.0 3.5 %all-to-all-start.2 = ((f32[16,4,2048]{2,0,1:T(8,128)}), f32[16,4,2048]{2,0,1:T(8,128)S(1)}, u32[]{:S(2)}, u32[]{:S(2)}) async-start(f32[16,4,2048]{2,0,1:T(8,128)} %copy.27), calls=%async_computation.2 | async-start | bytes 1048576 | tf_op jit(solution)/shard_map/all_to_all | solution.py:86
  66.4 7.9 %all-to-all-done.2 = f32[16,4,2048]{2,0,1:T(8,128)S(1)} async-done(((f32[16,4,2048]{2,0,1:T(8,128)}), f32[16,4,2048]{2,0,1:T(8,128)S(1)}, u32[]{:S(2)}, u32[]{:S(2)}) %all-to-all-start.2) | async-done | bytes 524320 | tf_op jit(solution)/shard_map/all_to_all | solution.py:86
  74.3 3.3 %all-to-all-start.4 = ((f32[1,8,128]{2,0,1:T(1,128)}), f32[1,8,128]{2,0,1:T(1,128)S(1)}, u32[]{:S(2)}, u32[]{:S(2)}) async-start(f32[1,8,128]{2,0,1:T(1,128)} %compare_select_fusion.1), calls=%async_computation.4 | async-start | bytes 8192 | tf_op jit(solution)/shard_map/all_to_all | solution.py:78
  77.6 1.4 %fusion.43 = f32[4,16,2048]{2,1,0:T(8,128)} fusion(f32[64,2048,1]{1,0,2:T(8,128)S(1)} %bitcast.57, f32[4,16]{1,0:T(4,128)S(1)} %div.34, s32[4,16]{1,0:T(4,128)S(1)} %le.27, s32[4,16]{1,0:T(4,128)S(1)} %ge.32, s32[4,16]{1,0:T(4,128)S(1)} %multiply_add_fusion), kind=kOutput, calls=%fused_computation.77 | convolution fusion | flops 100696064 | bytes 1049600 | tf_op jit(solution)/shard_map/dot_general | solution.py:63
  79.0 4.9 %all-to-all-done.4 = f32[1,8,128]{2,0,1:T(1,128)S(1)} async-done(((f32[1,8,128]{2,0,1:T(1,128)}), f32[1,8,128]{2,0,1:T(1,128)S(1)}, u32[]{:S(2)}, u32[]{:S(2)}) %all-to-all-start.4) | async-done | bytes 4128 | tf_op jit(solution)/shard_map/all_to_all | solution.py:78
  83.9 3.5 %all-to-all-start.3 = ((f32[4,16,2048]{2,1,0:T(8,128)}), f32[4,16,2048]{2,1,0:T(8,128)S(1)}, u32[]{:S(2)}, u32[]{:S(2)}) async-start(f32[4,16,2048]{2,1,0:T(8,128)} %fusion.43), calls=%async_computation.3 | async-start | bytes 1048576 | tf_op jit(solution)/shard_map/all_to_all | solution.py:87
  87.4 5.9 %scatter_custom_fusion.1 = f32[8192]{0:T(1024)S(1)} fusion(s32[1024]{0:T(1024)S(1)} %bitcast.64, f32[1024]{0:T(1024)S(1)} %bitcast.65, f32[]{:T(128)} %constant.2.clone.1), kind=kCustom, calls=%fused_computation.88 | custom fusion | flops 1024 | bytes 32772 | tf_op jit(solution)/shard_map/scatter-add | solution.py:85
  93.4 2.8 %all-to-all-done.3 = f32[4,16,2048]{2,1,0:T(8,128)S(1)} async-done(((f32[4,16,2048]{2,1,0:T(8,128)}), f32[4,16,2048]{2,1,0:T(8,128)S(1)}, u32[]{:S(2)}, u32[]{:S(2)}) %all-to-all-start.3) | async-done | bytes 524320 | tf_op jit(solution)/shard_map/all_to_all | solution.py:87
  97.0 2.5 %collective-permute-start = (f32[17,4,1024]{2,1,0:T(4,128)S(1)}, f32[17,4,1024]{2,1,0:T(4,128)S(1)}, u32[]{:S(2)}, u32[]{:S(2)}) collective-permute-start(f32[17,4,1024]{2,1,0:T(4,128)S(1)} %get-tuple-element.2), channel_id=1, source_target_pairs={{0,4},{4,8},{8,12},{12,16},{16,20},{20,24},{24,28},{1,5},{5,9},{9,... | collective-permute-start | bytes 835592 | tf_op jit(solution)/shard_map/ppermute | solution.py:22
  99.5 1.3 collective-permute-start.1
  100.8 10.3 %collective-permute-done = f32[17,4,1024]{2,1,0:T(4,128)S(1)} collective-permute-done((f32[17,4,1024]{2,1,0:T(4,128)S(1)}, f32[17,4,1024]{2,1,0:T(4,128)S(1)}, u32[]{:S(2)}, u32[]{:S(2)}) %collective-permute-start) | collective-permute-done | bytes 278560 | tf_op jit(solution)/shard_map/ppermute | solution.py:22
  113.5 2.7 %copy.29 = f32[16,8,1024]{0,2,1:T(8,128)} copy(f32[16,8,1024]{2,1,0:T(8,128)S(1)} %slice_divide_fusion) | data formatting | bytes 1048576 | tf_op jit(solution)/shard_map/div | solution.py:95
  116.2 5.0 %gather_fusion.3 = f32[1024,16]{1,0:T(8,128)S(1)} fusion(f32[16,8192]{0,1:T(8,128)} %bitcast.56, s32[1024]{0:T(1024)S(1)} %fusion.60), kind=kCustom, calls=%fused_computation.3 | custom fusion | bytes 135168 | tf_op jit(solution)/shard_map/gather | solution.py:97
  122.0 4.7 %all-to-all-start.5 = ((f32[16,8,128]{2,0,1:T(8,128)}), f32[16,8,128]{2,0,1:T(8,128)S(1)}, u32[]{:S(2)}, u32[]{:S(2)}) async-start(f32[16,8,128]{2,0,1:T(8,128)} %bitcast.22), calls=%async_computation.5 | async-start | bytes 131072 | tf_op jit(solution)/shard_map/all_to_all | solution.py:98
  126.7 6.8 %all-to-all-done.5 = f32[16,8,128]{2,0,1:T(8,128)S(1)} async-done(((f32[16,8,128]{2,0,1:T(8,128)}), f32[16,8,128]{2,0,1:T(8,128)S(1)}, u32[]{:S(2)}, u32[]{:S(2)}) %all-to-all-start.5) | async-done | bytes 65568 | tf_op jit(solution)/shard_map/all_to_all | solution.py:98
  (41 shorter events, 7.4 us)
Async XLA Ops:
  0.6 0.8 copy-start
  0.6 18.7 %copy-start.1 = (f32[16384]{0:T(1024)S(1)}, f32[16384]{0:T(1024)}, u32[]{:S(2)}) copy-start(f32[16384]{0:T(1024)} %param.7) | copy-start | bytes 196612
  1.5 24.0 %copy-start.3 = (f32[16,16384]{1,0:T(8,128)S(1)}, f32[16,16384]{1,0:T(8,128)}, u32[]{:S(2)}) copy-start(f32[16,16384]{1,0:T(8,128)} %param.6) | copy-start | bytes 3145732
  12.0 25.2 %all-to-all-start = ((s32[1,8,128]{2,0,1:T(1,128)}), s32[1,8,128]{2,0,1:T(1,128)S(1)}, u32[]{:S(2)}, u32[]{:S(2)}) async-start(s32[1,8,128]{2,0,1:T(1,128)} %bitcast.5), calls=%async_computation | async-start | bytes 8192 | tf_op jit(solution)/shard_map/all_to_all | solution.py:79
  25.5 11.0 %copy-start.4 = (s32[1,8]{1,0:T(1,128)S(1)}, s32[1,8]{1,0:T(1,128)}, u32[]{:S(2)}) copy-start(s32[1,8]{1,0:T(1,128)} %param.10) | copy-start | bytes 100
  37.2 12.9 %all-to-all-start.1 = ((f32[16,8,128]{2,0,1:T(8,128)}), f32[16,8,128]{2,0,1:T(8,128)S(1)}, u32[]{:S(2)}, u32[]{:S(2)}) async-start(f32[16,8,128]{2,0,1:T(8,128)} %bitcast_multiply_fusion), calls=%async_computation.1 | async-start | bytes 131072 | tf_op jit(solution)/shard_map/all_to_all | solution.py:77
  50.3 15.2 %copy-start.5 = (s32[64]{0:T(128)S(1)}, s32[64]{0:T(128)}, u32[]{:S(2)}) copy-start(s32[64]{0:T(128)} %param.11) | copy-start | bytes 772
  62.0 12.3 %all-to-all-start.2 = ((f32[16,4,2048]{2,0,1:T(8,128)}), f32[16,4,2048]{2,0,1:T(8,128)S(1)}, u32[]{:S(2)}, u32[]{:S(2)}) async-start(f32[16,4,2048]{2,0,1:T(8,128)} %copy.27), calls=%async_computation.2 | async-start | bytes 1048576 | tf_op jit(solution)/shard_map/all_to_all | solution.py:86
  74.3 9.6 %all-to-all-start.4 = ((f32[1,8,128]{2,0,1:T(1,128)}), f32[1,8,128]{2,0,1:T(1,128)S(1)}, u32[]{:S(2)}, u32[]{:S(2)}) async-start(f32[1,8,128]{2,0,1:T(1,128)} %compare_select_fusion.1), calls=%async_computation.4 | async-start | bytes 8192 | tf_op jit(solution)/shard_map/all_to_all | solution.py:78
  83.9 12.3 %all-to-all-start.3 = ((f32[4,16,2048]{2,1,0:T(8,128)}), f32[4,16,2048]{2,1,0:T(8,128)S(1)}, u32[]{:S(2)}, u32[]{:S(2)}) async-start(f32[4,16,2048]{2,1,0:T(8,128)} %fusion.43), calls=%async_computation.3 | async-start | bytes 1048576 | tf_op jit(solution)/shard_map/all_to_all | solution.py:87
  97.0 14.1 %collective-permute-start = (f32[17,4,1024]{2,1,0:T(4,128)S(1)}, f32[17,4,1024]{2,1,0:T(4,128)S(1)}, u32[]{:S(2)}, u32[]{:S(2)}) collective-permute-start(f32[17,4,1024]{2,1,0:T(4,128)S(1)} %get-tuple-element.2), channel_id=1, source_target_pairs={{0,4},{4,8},{8,12},{12,16},{16,20},{20,24},{24,28},{1,5},{5,9},{9,... | collective-permute-start | bytes 835592 | tf_op jit(solution)/shard_map/ppermute | solution.py:22
  99.5 11.7 %collective-permute-start.1 = (f32[17,4,1024]{2,1,0:T(4,128)S(1)}, f32[17,4,1024]{2,1,0:T(4,128)S(1)}, u32[]{:S(2)}, u32[]{:S(2)}) collective-permute-start(f32[17,4,1024]{2,1,0:T(4,128)S(1)} %get-tuple-element.3), channel_id=1, source_target_pairs={{4,0},{8,4},{12,8},{16,12},{20,16},{24,20},{28,24},{5,1},{9,5},{13... | collective-permute-start | bytes 835592 | tf_op jit(solution)/shard_map/ppermute | solution.py:24
  113.5 20.7 %copy-start.2 = (f32[16,8,1024]{2,1,0:T(8,128)}, f32[16,8,1024]{2,1,0:T(8,128)S(1)}, u32[]{:S(2)}) copy-start(f32[16,8,1024]{2,1,0:T(8,128)S(1)} %slice_divide_fusion) | copy-start | bytes 1572868
  122.0 11.6 %all-to-all-start.5 = ((f32[16,8,128]{2,0,1:T(8,128)}), f32[16,8,128]{2,0,1:T(8,128)S(1)}, u32[]{:S(2)}, u32[]{:S(2)}) async-start(f32[16,8,128]{2,0,1:T(8,128)} %bitcast.22), calls=%async_computation.5 | async-start | bytes 131072 | tf_op jit(solution)/shard_map/all_to_all | solution.py:98
where the time goes:
time: 135 us; the launch traced here: 134 us
  local copies, waits for them, and re-layouts  40.9 us (30%)
  waiting for transfers between devices  39.7 us (29%)
  starting transfers between devices  31.9 us (24%)
  other arithmetic  19.3 us (14%)
  matrix products  1.42 us (1%)
    gather x1, local copies, waits for them, and re-layouts, shards(): slot_pixel = pixel_index[send_list]  10.5 us
    ppermute x1, waiting for transfers between devices, with_halo(): lax.ppermute(tail, axis, [(i, (i + 1) % count) for i in range(ends)])  10.3 us
    scatter-add x1, other arithmetic, shards(): jnp.zeros((acq_loc, SLAB_PIX), jnp.float32).at[:, targets]  8.21 us
    all_to_all x1, waiting for transfers between devices, shards(): lax.all_to_all(phase_image, 'acq', split_axis=1, concat_axis=0, tiled=True)  7.86 us
    all_to_all x1, starting transfers between devices, shards(): lax.all_to_all(slot_pixel[None], 'tile', split_axis=1, concat_axis=1, til...  7.28 us
    all_to_all x1, waiting for transfers between devices, shards(): lax.all_to_all(outgoing, 'tile', split_axis=1, concat_axis=1, tiled=True)  6.9 us
    all_to_all x1, waiting for transfers between devices, shards(): lax.all_to_all(sampled, 'tile', split_axis=1, concat_axis=1, tiled=True)  6.83 us
    gather x2, local copies, waits for them, and re-layouts, shards(): phases[:, send_list] - returned  6.35 us
  transfers between devices with their start and end apart: 8, of which 6 were waited for; matrix products, arithmetic and copies ran while one was open for 20% of the time, Pallas kernels for 0%

commit v1 on v0

--- a/solution.py
+++ b/solution.py
@@ -9,6 +9,22 @@
 RADIUS = 4
 SLAB_PIX = 8192
 min_weight = 0.1
+
+
+def fix_sites_now(in_array, pos_dim, field):
+    reply = in_array.shape
+    raw_out = in_array.reshape(
+        *reply[:pos_dim], field, reply[pos_dim] // field, *reply[pos_dim + 1 :]
+    )
+    return jnp.moveaxis(raw_out, pos_dim, 0)
+
+
+def settle_numbers_on_mesh(piece_in, array_dim):
+    piece_in = jnp.moveaxis(piece_in, 0, array_dim)
+    clean = piece_in.shape
+    return piece_in.reshape(
+        *clean[:array_dim], clean[array_dim] * clean[array_dim + 1], *clean[array_dim + 2 :]
+    )
 
 
 def with_halo(cells, sides, width):
@@ -66,6 +82,23 @@
 
 
 def shards(phases, coherence, pixel_index, send_list, counts, band_width):
+
+    def handle_node(x_in, shard_axis, array_in, vec):
+        h_now = lax.axis_index(shard_axis)
+        y2 = lax.axis_size(shard_axis)
+        low, w2 = (y2, h_now)
+        spare = fix_sites_now(x_in, array_in, low)
+        shelf = [spare[w2]]
+        for t in range(1, low):
+            local_out = spare[w2 ^ t]
+            answer = lax.ppermute(
+                local_out, axis_name=shard_axis, perm=[(s, s ^ t) for s in range(low)]
+            )
+            shelf.append(answer)
+        t_next = jnp.stack(shelf)
+        spare = t_next[w2 ^ jnp.arange(low)]
+        return settle_numbers_on_mesh(spare, vec)
+
     acq_loc = phases.shape[0]
     capacity = send_list.shape[1]
     highpass = temporal_matrix(band_width)
@@ -84,9 +117,7 @@
     )
     weight_sum = jnp.zeros((SLAB_PIX,), jnp.float32).at[targets].add(arrived_weight.reshape(-1))
     series = lax.all_to_all(phase_image, "acq", split_axis=1, concat_axis=0, tiled=True)
-    phase_image = lax.all_to_all(
-        apply_highpass(highpass, series), "acq", split_axis=0, concat_axis=1, tiled=True
-    )
+    phase_image = handle_node(apply_highpass(highpass, series), "acq", 0, 1)
     stacked = jnp.concatenate([phase_image, weight_sum[None, :]], axis=0).reshape(
         acq_loc + 1, ROWS_DEV, COLS
     )

time: 135 us -> 129 us (0.956)
  waiting for transfers between devices: 39.7 us -> 33.3 us
    ppermute x1, waiting for transfers between devices: 10.3 us -> 4.94 us  [with_halo(): lax.ppermute(tail, axis, [(i, (i + 1) % count) for i in range(ends)])]
    all_to_all x1 -> x0, starting transfers between devices: 3.47 us -> none  [shards(): lax.all_to_all(apply_highpass(highpass, series), 'acq', split_axis=0, con...]
    ppermute x1, waiting for transfers between devices: 0.01 us -> 3.06 us  [with_halo(): lax.ppermute(head, axis, [((i + 1) % count, i) for i in range(ends)])]
    all_to_all x1 -> x0, waiting for transfers between devices: 2.84 us -> none  [shards(): lax.all_to_all(apply_highpass(highpass, series), 'acq', split_axis=0, con...]
    ppermute x1, starting transfers between devices: 2.47 us -> 4.56 us  [with_halo(): lax.ppermute(tail, axis, [(i, (i + 1) % count) for i in range(ends)])]
    ppermute x0 -> x3, starting transfers between devices: none -> 1.92 us  [handle_node(): lax.ppermute(local_out, axis_name=shard_axis, perm=[(s, s ^ t) for s in r...]
  transfers between devices with their start and end apart: 8 -> 10, of which waited for: 6 -> 6; matrix products, arithmetic and copies ran while one was open for 20% -> 20% of each run, Pallas kernels for 0% -> 0%
where the time goes in v1:
time: 129 us; the launch traced here: 128 us
  local copies, waits for them, and re-layouts  41.5 us (32%)
  waiting for transfers between devices  33.3 us (26%)
  starting transfers between devices  32.7 us (25%)
  other arithmetic  19.4 us (15%)
    gather x1, local copies, waits for them, and re-layouts, shards(): slot_pixel = pixel_index[send_list]  10.5 us
    scatter-add x1, other arithmetic, shards(): jnp.zeros((acq_loc, SLAB_PIX), jnp.float32).at[:, targets]  8.2 us
    all_to_all x1, waiting for transfers between devices, shards(): lax.all_to_all(phase_image, 'acq', split_axis=1, concat_axis=0, tiled=True)  7.85 us
    all_to_all x1, starting transfers between devices, shards(): lax.all_to_all(slot_pixel[None], 'tile', split_axis=1, concat_axis=1, til...  7.28 us
    all_to_all x1, waiting for transfers between devices, shards(): lax.all_to_all(outgoing, 'tile', split_axis=1, concat_axis=1, tiled=True)  6.9 us
    all_to_all x1, waiting for transfers between devices, shards(): lax.all_to_all(sampled, 'tile', split_axis=1, concat_axis=1, tiled=True)  6.83 us
    gather x2, local copies, waits for them, and re-layouts, shards(): phases[:, send_list] - returned  6.36 us
    gather x1, local copies, waits for them, and re-layouts, shards(): slot_weight = jnp.where(live_slot, coherence[send_list], jnp.float32(0.0))  6.16 us
  transfers between devices with their start and end apart: 10, of which 6 were waited for; matrix products, arithmetic and copies ran while one was open for 20% of the time, Pallas kernels for 0%

profile of v1, /device:TPU:0, one launch (start us, length us, event | category | flops | bytes accessed | tf_op | source)
XLA Modules:
  0.0 128.4 jit_solution(2649015451825769976)
XLA Ops:
  1.5 10.5 %gather_fusion.1 = s32[1024]{0:T(1024)} fusion(s32[16384]{0:T(1024)S(1)} %copy-done, s32[1024]{0:T(1024)S(1)} %fusion.58), kind=kCustom, calls=%fused_computation.1 | custom fusion | bytes 12288 | tf_op jit(solution)/shard_map/gather | solution.py:107
  12.0 7.3 %all-to-all-start = ((s32[1,8,128]{2,0,1:T(1,128)}), s32[1,8,128]{2,0,1:T(1,128)S(1)}, u32[]{:S(2)}, u32[]{:S(2)}) async-start(s32[1,8,128]{2,0,1:T(1,128)} %bitcast.5), calls=%async_computation | async-start | bytes 8192 | tf_op jit(solution)/shard_map/all_to_all | solution.py:112
  19.3 4.6 %copy.23 = f32[16,16384]{0,1:T(8,128)} copy(f32[16,16384]{1,0:T(8,128)S(1)} %copy-done.3) | data formatting | bytes 2097152 | tf_op args[0]
  23.9 6.2 %gather_fusion = f32[1024,16]{1,0:T(8,128)S(1)} fusion(f32[16,16384]{0,1:T(8,128)} %copy.23, s32[1024]{0:T(1024)S(1)} %fusion.58), kind=kCustom, calls=%fused_computation | custom fusion | bytes 135168 | tf_op jit(solution)/shard_map/gather | solution.py:130
  30.3 6.2 %gather_fusion.2 = f32[1024]{0:T(1024)S(1)} fusion(f32[16384]{0:T(1024)S(1)} %copy-done.1, s32[1024]{0:T(1024)S(1)} %fusion.58), kind=kCustom, calls=%fused_computation.2 | custom fusion | bytes 12288 | tf_op jit(solution)/shard_map/gather | solution.py:106
  37.2 6.0 %all-to-all-start.1 = ((f32[16,8,128]{2,0,1:T(8,128)}), f32[16,8,128]{2,0,1:T(8,128)S(1)}, u32[]{:S(2)}, u32[]{:S(2)}) async-start(f32[16,8,128]{2,0,1:T(8,128)} %bitcast_multiply_fusion), calls=%async_computation.1 | async-start | bytes 131072 | tf_op jit(solution)/shard_map/all_to_all | solution.py:110
  43.2 6.9 %all-to-all-done.1 = f32[16,8,128]{2,0,1:T(8,128)S(1)} async-done(((f32[16,8,128]{2,0,1:T(8,128)}), f32[16,8,128]{2,0,1:T(8,128)S(1)}, u32[]{:S(2)}, u32[]{:S(2)}) %all-to-all-start.1) | async-done | bytes 65568 | tf_op jit(solution)/shard_map/all_to_all | solution.py:110
  50.3 8.2 %scatter_custom_fusion = f32[16,8192]{0,1:T(8,128)} fusion(s32[1024]{0:T(1024)S(1)} %bitcast.77, f32[1024,16]{1,0:T(8,128)S(1)} %copy.26, f32[]{:T(128)} %constant.22.clone.1), kind=kCustom, calls=%fused_computation.7 | custom fusion | flops 16384 | bytes 524292 | tf_op jit(solution)/shard_map/scatter-add | solution.py:116
  58.5 3.5 %copy.27 = f32[16,4,2048]{2,0,1:T(8,128)} copy(f32[16,4,2048]{0,2,1:T(8,128)} %bitcast.66) | data formatting | bytes 1048576 | tf_op jit(solution)/shard_map/all_to_all | solution.py:119
  62.0 3.5 %all-to-all-start.2 = ((f32[16,4,2048]{2,0,1:T(8,128)}), f32[16,4,2048]{2,0,1:T(8,128)S(1)}, u32[]{:S(2)}, u32[]{:S(2)}) async-start(f32[16,4,2048]{2,0,1:T(8,128)} %copy.27), calls=%async_computation.2 | async-start | bytes 1048576 | tf_op jit(solution)/shard_map/all_to_all | solution.py:119
  66.4 7.8 %all-to-all-done.2 = f32[16,4,2048]{2,0,1:T(8,128)S(1)} async-done(((f32[16,4,2048]{2,0,1:T(8,128)}), f32[16,4,2048]{2,0,1:T(8,128)S(1)}, u32[]{:S(2)}, u32[]{:S(2)}) %all-to-all-start.2) | async-done | bytes 524320 | tf_op jit(solution)/shard_map/all_to_all | solution.py:119
  74.3 3.3 %all-to-all-start.3 = ((f32[1,8,128]{2,0,1:T(1,128)}), f32[1,8,128]{2,0,1:T(1,128)S(1)}, u32[]{:S(2)}, u32[]{:S(2)}) async-start(f32[1,8,128]{2,0,1:T(1,128)} %compare_select_fusion.1), calls=%async_computation.3 | async-start | bytes 8192 | tf_op jit(solution)/shard_map/all_to_all | solution.py:111
  78.4 1.3 collective-permute-start.1
  80.2 3.7 %all-to-all-done.3 = f32[1,8,128]{2,0,1:T(1,128)S(1)} async-done(((f32[1,8,128]{2,0,1:T(1,128)}), f32[1,8,128]{2,0,1:T(1,128)S(1)}, u32[]{:S(2)}, u32[]{:S(2)}) %all-to-all-start.3) | async-done | bytes 4128 | tf_op jit(solution)/shard_map/all_to_all | solution.py:111
  83.9 5.9 %scatter_custom_fusion.1 = f32[8192]{0:T(1024)S(1)} fusion(s32[1024]{0:T(1024)S(1)} %bitcast.78, f32[1024]{0:T(1024)S(1)} %bitcast.79, f32[]{:T(128)} %constant.22.clone.1), kind=kCustom, calls=%fused_computation.93 | custom fusion | flops 1024 | bytes 32772 | tf_op jit(solution)/shard_map/scatter-add | solution.py:118
  91.3 1.3 %collective-permute-start.4 = (f32[17,4,1024]{2,1,0:T(4,128)S(1)}, f32[17,4,1024]{2,1,0:T(4,128)S(1)}, u32[]{:S(2)}, u32[]{:S(2)}) collective-permute-start(f32[17,4,1024]{2,1,0:T(4,128)S(1)} %get-tuple-element.3), channel_id=1, source_target_pairs={{4,0},{8,4},{12,8},{16,12},{20,16},{24,20},{28,24},{5,1},{9,5},{13... | collective-permute-start | bytes 835592 | tf_op jit(solution)/shard_map/ppermute | solution.py:40
  92.6 4.6 %collective-permute-start.3 = (f32[17,4,1024]{2,1,0:T(4,128)S(1)}, f32[17,4,1024]{2,1,0:T(4,128)S(1)}, u32[]{:S(2)}, u32[]{:S(2)}) collective-permute-start(f32[17,4,1024]{2,1,0:T(4,128)S(1)} %get-tuple-element.2), channel_id=1, source_target_pairs={{0,4},{4,8},{8,12},{12,16},{16,20},{20,24},{24,28},{1,5},{5,9},{9,... | collective-permute-start | bytes 835592 | tf_op jit(solution)/shard_map/ppermute | solution.py:38
  97.2 3.1 %collective-permute-done.4 = f32[17,4,1024]{2,1,0:T(4,128)S(1)} collective-permute-done((f32[17,4,1024]{2,1,0:T(4,128)S(1)}, f32[17,4,1024]{2,1,0:T(4,128)S(1)}, u32[]{:S(2)}, u32[]{:S(2)}) %collective-permute-start.4) | collective-permute-done | bytes 278560 | tf_op jit(solution)/shard_map/ppermute | solution.py:40
  100.3 4.9 %collective-permute-done.3 = f32[17,4,1024]{2,1,0:T(4,128)S(1)} collective-permute-done((f32[17,4,1024]{2,1,0:T(4,128)S(1)}, f32[17,4,1024]{2,1,0:T(4,128)S(1)}, u32[]{:S(2)}, u32[]{:S(2)}) %collective-permute-start.3) | collective-permute-done | bytes 278560 | tf_op jit(solution)/shard_map/ppermute | solution.py:38
  106.2 1.2 fusion.10
  107.6 2.7 %copy.29 = f32[16,8,1024]{0,2,1:T(8,128)} copy(f32[16,8,1024]{2,1,0:T(8,128)S(1)} %slice_divide_fusion) | data formatting | bytes 1048576 | tf_op jit(solution)/shard_map/div | solution.py:126
  110.2 5.0 %gather_fusion.4 = f32[1024,16]{1,0:T(8,128)S(1)} fusion(f32[16,8192]{0,1:T(8,128)} %bitcast.67, s32[1024]{0:T(1024)S(1)} %fusion.60), kind=kCustom, calls=%fused_computation.4 | custom fusion | bytes 135168 | tf_op jit(solution)/shard_map/gather | solution.py:128
  116.0 4.8 %all-to-all-start.4 = ((f32[16,8,128]{2,0,1:T(8,128)}), f32[16,8,128]{2,0,1:T(8,128)S(1)}, u32[]{:S(2)}, u32[]{:S(2)}) async-start(f32[16,8,128]{2,0,1:T(8,128)} %bitcast.29), calls=%async_computation.4 | async-start | bytes 131072 | tf_op jit(solution)/shard_map/all_to_all | solution.py:129
  121.0 6.8 %all-to-all-done.4 = f32[16,8,128]{2,0,1:T(8,128)S(1)} async-done(((f32[16,8,128]{2,0,1:T(8,128)}), f32[16,8,128]{2,0,1:T(8,128)S(1)}, u32[]{:S(2)}, u32[]{:S(2)}) %all-to-all-start.4) | async-done | bytes 65568 | tf_op jit(solution)/shard_map/all_to_all | solution.py:129
  (50 shorter events, 8.2 us)
Async XLA Ops:
  0.6 0.8 copy-start
  0.6 18.7 %copy-start.3 = (f32[16,16384]{1,0:T(8,128)S(1)}, f32[16,16384]{1,0:T(8,128)}, u32[]{:S(2)}) copy-start(f32[16,16384]{1,0:T(8,128)} %param.6) | copy-start | bytes 3145732
  12.0 25.2 %all-to-all-start = ((s32[1,8,128]{2,0,1:T(1,128)}), s32[1,8,128]{2,0,1:T(1,128)S(1)}, u32[]{:S(2)}, u32[]{:S(2)}) async-start(s32[1,8,128]{2,0,1:T(1,128)} %bitcast.5), calls=%async_computation | async-start | bytes 8192 | tf_op jit(solution)/shard_map/all_to_all | solution.py:112
  19.3 11.0 %copy-start.1 = (f32[16384]{0:T(1024)S(1)}, f32[16384]{0:T(1024)}, u32[]{:S(2)}) copy-start(f32[16384]{0:T(1024)} %param.7) | copy-start | bytes 196612
  23.9 12.5 %copy-start.4 = (s32[1,8]{1,0:T(1,128)S(1)}, s32[1,8]{1,0:T(1,128)}, u32[]{:S(2)}) copy-start(s32[1,8]{1,0:T(1,128)} %param.10) | copy-start | bytes 100
  37.2 12.9 %all-to-all-start.1 = ((f32[16,8,128]{2,0,1:T(8,128)}), f32[16,8,128]{2,0,1:T(8,128)S(1)}, u32[]{:S(2)}, u32[]{:S(2)}) async-start(f32[16,8,128]{2,0,1:T(8,128)} %bitcast_multiply_fusion), calls=%async_computation.1 | async-start | bytes 131072 | tf_op jit(solution)/shard_map/all_to_all | solution.py:110
  50.3 15.2 %copy-start.5 = (s32[64]{0:T(128)S(1)}, s32[64]{0:T(128)}, u32[]{:S(2)}) copy-start(s32[64]{0:T(128)} %param.11) | copy-start | bytes 772
  62.0 12.3 %all-to-all-start.2 = ((f32[16,4,2048]{2,0,1:T(8,128)}), f32[16,4,2048]{2,0,1:T(8,128)S(1)}, u32[]{:S(2)}, u32[]{:S(2)}) async-start(f32[16,4,2048]{2,0,1:T(8,128)} %copy.27), calls=%async_computation.2 | async-start | bytes 1048576 | tf_op jit(solution)/shard_map/all_to_all | solution.py:119
  74.3 9.6 %all-to-all-start.3 = ((f32[1,8,128]{2,0,1:T(1,128)}), f32[1,8,128]{2,0,1:T(1,128)S(1)}, u32[]{:S(2)}, u32[]{:S(2)}) async-start(f32[1,8,128]{2,0,1:T(1,128)} %compare_select_fusion.1), calls=%async_computation.3 | async-start | bytes 8192 | tf_op jit(solution)/shard_map/all_to_all | solution.py:111
  78.3 11.6 %collective-permute-start.2 = (f32[16,2048]{1,0:T(8,128)S(1)}, f32[16,2048]{1,0:T(8,128)S(1)}, u32[]{:S(2)}, u32[]{:S(2)}) collective-permute-start(f32[16,2048]{1,0:T(8,128)S(1)} %get-tuple-element.5), channel_id=1, source_target_pairs={{0,3},{1,2},{2,1},{3,0},{4,7},{5,6},{6,5},{7,4},{8,11},{9,10},{10,... | collective-permute-start | bytes 393224 | tf_op jit(solution)/shard_map/ppermute | solution.py:94
  78.4 11.5 %collective-permute-start.1 = (f32[16,2048]{1,0:T(8,128)S(1)}, f32[16,2048]{1,0:T(8,128)S(1)}, u32[]{:S(2)}, u32[]{:S(2)}) collective-permute-start(f32[16,2048]{1,0:T(8,128)S(1)} %get-tuple-element.6), channel_id=1, source_target_pairs={{0,2},{1,3},{2,0},{3,1},{4,6},{5,7},{6,4},{7,5},{8,10},{9,11},{10,... | collective-permute-start | bytes 393224 | tf_op jit(solution)/shard_map/ppermute | solution.py:94
  79.6 10.3 %collective-permute-start = (f32[16,2048]{1,0:T(8,128)S(1)}, f32[16,2048]{1,0:T(8,128)S(1)}, u32[]{:S(2)}, u32[]{:S(2)}) collective-permute-start(f32[16,2048]{1,0:T(8,128)S(1)} %get-tuple-element.7), channel_id=1, source_target_pairs={{0,1},{1,0},{2,3},{3,2},{4,5},{5,4},{6,7},{7,6},{8,9},{9,8},{10,11... | collective-permute-start | bytes 393224 | tf_op jit(solution)/shard_map/ppermute | solution.py:94
  91.3 8.9 %collective-permute-start.4 = (f32[17,4,1024]{2,1,0:T(4,128)S(1)}, f32[17,4,1024]{2,1,0:T(4,128)S(1)}, u32[]{:S(2)}, u32[]{:S(2)}) collective-permute-start(f32[17,4,1024]{2,1,0:T(4,128)S(1)} %get-tuple-element.3), channel_id=1, source_target_pairs={{4,0},{8,4},{12,8},{16,12},{20,16},{24,20},{28,24},{5,1},{9,5},{13... | collective-permute-start | bytes 835592 | tf_op jit(solution)/shard_map/ppermute | solution.py:40
  92.6 12.6 %collective-permute-start.3 = (f32[17,4,1024]{2,1,0:T(4,128)S(1)}, f32[17,4,1024]{2,1,0:T(4,128)S(1)}, u32[]{:S(2)}, u32[]{:S(2)}) collective-permute-start(f32[17,4,1024]{2,1,0:T(4,128)S(1)} %get-tuple-element.2), channel_id=1, source_target_pairs={{0,4},{4,8},{8,12},{12,16},{16,20},{20,24},{24,28},{1,5},{5,9},{9,... | collective-permute-start | bytes 835592 | tf_op jit(solution)/shard_map/ppermute | solution.py:38
  107.5 20.9 %copy-start.2 = (f32[16,8,1024]{2,1,0:T(8,128)}, f32[16,8,1024]{2,1,0:T(8,128)S(1)}, u32[]{:S(2)}) copy-start(f32[16,8,1024]{2,1,0:T(8,128)S(1)} %slice_divide_fusion) | copy-start | bytes 1572868
  116.0 11.8 %all-to-all-start.4 = ((f32[16,8,128]{2,0,1:T(8,128)}), f32[16,8,128]{2,0,1:T(8,128)S(1)}, u32[]{:S(2)}, u32[]{:S(2)}) async-start(f32[16,8,128]{2,0,1:T(8,128)} %bitcast.29), calls=%async_computation.4 | async-start | bytes 131072 | tf_op jit(solution)/shard_map/all_to_all | solution.py:129
